TPU v7x, 512 devices: a whole 4x8x8 slice. The times are simulated.
512 devices in a mesh: grp: 16 (over y, x_hi), pos: 32 (over x_lo, z, core).
Axes of the slice: x: 4 (x_hi: 2, x_lo: 2; x = x_hi * 2 + x_lo), y: 8, z: 8, core: 2. Of those that a mesh axis runs over, the one named last changes fastest.
Arguments:
- features: bfloat16 [2, 2048, 512, 448], P(None, ('grp', 'pos'))
- channel_index: int32 [100], replicated, may hold values from 0 to 447, as said below
Outputs:
- factor: float32 [512, 100, 100], P('pos')
- mean_vec: float32 [512, 100], P('pos')
Inputs may be any that keep to these rules, and one draw needn't show every extreme that they name: `channel_index`: 100 distinct channel numbers; 0 and 447 are always among them.
All inputs are finite; a program needn't handle non-finite values.
Results may differ from a plain program's by a relative error of at most 0.0003.
Values may be sent and summed in bfloat16 or wider, within the bound.
A program may use at most 64 MiB of HBM per device.

v0:
```python
import jax
import jax.numpy as jnp
from jax import lax
from jax.sharding import PartitionSpec as P

RIDGE = 0.01


def moments(received):
    samples = received.reshape(received.shape[0], received.shape[2], received.shape[3])
    second_moment = jnp.einsum("ipc,ipd->pcd", samples, samples, preferred_element_type=jnp.float32)
    column_sums = jnp.sum(samples.astype(jnp.float32), axis=0)
    return (second_moment, column_sums)


def combine(second_moment, column_sums):
    return (
        lax.psum_scatter(second_moment, "grp", scatter_dimension=0, tiled=True),
        lax.psum_scatter(column_sums, "grp", scatter_dimension=0, tiled=True),
    )


def factorize(second_moment, column_sums, image_total):
    mean_vec = column_sums / image_total
    outer = image_total * mean_vec[:, :, None] * mean_vec[:, None, :]
    identity = jnp.eye(mean_vec.shape[1], dtype=jnp.float32)
    covariance = (second_moment - outer) / (image_total - 1) + RIDGE * identity
    return (jnp.linalg.cholesky(covariance), mean_vec)


def local(features, channel_index):
    pos_count = lax.axis_size("pos")
    grp_count = lax.axis_size("grp")
    batch_total, img_local, positions, width = features.shape
    keep_count = channel_index.shape[0]
    selector = (
        lax.broadcasted_iota(jnp.int32, (width, keep_count), 0) == channel_index[None, :]
    ).astype(jnp.bfloat16)
    image_total = batch_total * img_local * pos_count * grp_count
    chosen_list = []
    for batch_index in range(batch_total):
        flat = features[batch_index].reshape(img_local * positions, width)
        chosen = jnp.dot(flat, selector, preferred_element_type=jnp.float32).astype(jnp.bfloat16)
        chosen_list.append(chosen)
    partial_list = []
    for chosen in chosen_list:
        shaped = chosen.reshape(img_local, pos_count, positions // pos_count, keep_count)
        partial_list.append(
            moments(lax.all_to_all(shaped, "pos", split_axis=1, concat_axis=0, tiled=True))
        )
    shares = [combine(pair[0], pair[1]) for pair in partial_list]
    second_moment = shares[0][0]
    column_sums = shares[0][1]
    for pair in shares[1:]:
        second_moment = second_moment + pair[0]
        column_sums = column_sums + pair[1]
    factor, mean_vec = factorize(second_moment, column_sums, image_total)
    factor, mean_vec = (
        lax.all_gather(factor, "grp", axis=0, tiled=True),
        lax.all_gather(mean_vec, "grp", axis=0, tiled=True),
    )
    return (factor, mean_vec)


def solution(mesh):
    return jax.shard_map(
        local,
        mesh=mesh,
        in_specs=(P(None, ("grp", "pos"), None, None), P()),
        out_specs=(P("pos", None, None), P("pos", None)),
        check_vma=False,
    )
```

profile of v0, /device:TPU:64, one launch (start us, length us, event | category | flops | bytes accessed | tf_op | source)
XLA Modules:
  0.0 289.7 jit_solution(10344877939015737435)
XLA Ops:
  7.2 2.4 fusion.10
  9.6 1.4 copy.28
  11.0 0.0 copy-start
  11.0 0.5 copy.44
  11.5 0.1 copy-done
  11.7 0.5 fusion
  12.1 0.3 copy.29
  12.4 0.9 copy.30
  13.3 11.1 %all-to-all-start = ((bf16[4,32,16,100]{3,2,0,1:T(8,128)(2,1)}), bf16[4,32,16,100]{3,2,0,1:T(8,128)(2,1)S(1)}, u32[]{:S(2)}, u32[]{:S(2)}) async-start(bf16[4,32,16,100]{3,2,0,1:T(8,128)(2,1)} %copy.30), calls=%async_computation | async-start | bytes 1048576 | tf_op jit(solution)/shard_map/all_to_all | solution.py:49
  24.3 1.4 copy.33
  25.7 0.5 copy.45
  26.3 0.5 fusion.1
  26.7 0.3 copy.34
  27.0 0.9 copy.35
  27.9 14.2 %all-to-all-done = bf16[4,32,16,100]{3,2,0,1:T(8,128)(2,1)S(1)} async-done(((bf16[4,32,16,100]{3,2,0,1:T(8,128)(2,1)}), bf16[4,32,16,100]{3,2,0,1:T(8,128)(2,1)S(1)}, u32[]{:S(2)}, u32[]{:S(2)}) %all-to-all-start) | async-done | bytes 409632 | tf_op jit(solution)/shard_map/all_to_all | solution.py:49
  42.1 4.5 %all-to-all-start.1 = ((bf16[4,32,16,100]{3,2,0,1:T(8,128)(2,1)}), bf16[4,32,16,100]{3,2,0,1:T(8,128)(2,1)S(1)}, u32[]{:S(2)}, u32[]{:S(2)}) async-start(bf16[4,32,16,100]{3,2,0,1:T(8,128)(2,1)} %copy.35), calls=%async_computation.1 | async-start | bytes 1048576 | tf_op jit(solution)/shard_map/all_to_all | solution.py:49
  46.6 0.0 reduce-scatter.4.cloned.1.call-start
  46.6 0.4 fusion.3
  47.0 17.4 %all-to-all-done.1 = bf16[4,32,16,100]{3,2,0,1:T(8,128)(2,1)S(1)} async-done(((bf16[4,32,16,100]{3,2,0,1:T(8,128)(2,1)}), bf16[4,32,16,100]{3,2,0,1:T(8,128)(2,1)S(1)}, u32[]{:S(2)}, u32[]{:S(2)}) %all-to-all-start.1) | async-done | bytes 409632 | tf_op jit(solution)/shard_map/all_to_all | solution.py:49
  64.4 0.4 convolution_add_fusion
  64.9 1.2 copy.38
  66.1 0.0 reduce-scatter.4.cloned.1.call-update
  66.1 1.3 dynamic-slice
  67.4 0.2 convert_reduce_fusion
  67.6 0.2 convert_reduce_fusion.1
  67.7 42.8 %all-reduce.1 = f32[16,100]{1,0:T(8,128)S(1)} all-reduce(f32[16,100]{1,0:T(8,128)S(1)} %add.31), channel_id=5, replica_groups=mesh['grp'=16,'pos'=32] {'grp'}, use_global_device_ids=true, to_apply=%region_3.0.clone | all-reduce | flops 1600 | bytes 12800
  110.5 0.7 fusion.8
  111.2 35.3 %all-gather = f32[16,1,100]{2,1,0:T(1,128)S(1)} all-gather(f32[1,1,100]{2,1,0:T(1,128)S(1)} %get-tuple-element.10), channel_id=1, replica_groups=mesh['grp'=16,'pos'=32] {'grp'}, dimensions={0}, use_global_device_ids=true | all-gather | bytes 6800 | tf_op jit(solution)/shard_map/all_gather | solution.py:60
  146.5 0.7 broadcast_multiply_fusion
  147.2 78.3 %reduce-scatter.4.cloned.1.call-done = f32[1,100,100]{1,2,0:T(8,128)} async-done(((f32[16,100,100]{1,2,0:T(8,128)}), f32[1,100,100]{1,2,0:T(8,128)}) %reduce-scatter.4.cloned.1.call-update) | async-done | bytes 40016
  225.5 0.9 select_add_fusion
  226.4 0.1 copy.39
  226.5 0.9 fusion.7
  227.4 9.1 %custom-call.4 = f32[1,100,100]{2,1,0:T(8,128)S(1)} custom-call(f32[1,100,100]{2,1,0:T(8,128)S(1)} %fusion.7), custom_call_target="Cholesky" | custom-call | tf_op jit(solution)/shard_map/jit(cholesky)/cholesky | solution.py:28
  236.6 0.1 copy.40
  236.7 0.1 select_reduce_fusion
  236.8 0.6 compare_reduce_fusion
  237.4 0.7 select_select_fusion
  238.1 0.1 copy.42
  238.2 43.0 %all_gather.6 = f32[16,100,100]{2,1,0:T(8,128)S(1)} all-gather(f32[1,100,100]{2,1,0:T(8,128)S(1)} %copy.42), channel_id=1, replica_groups=mesh['grp'=16,'pos'=32] {'grp'}, dimensions={0}, use_global_device_ids=true | all-gather | bytes 680000 | tf_op jit(solution)/shard_map/all_gather | solution.py:59
  281.2 1.0 copy.43
  282.3 0.6 copy.51
  (1 shorter events, 0.0 us)
Async XLA Ops:
  11.0 0.7 copy-start
  13.3 28.8 %all-to-all-start = ((bf16[4,32,16,100]{3,2,0,1:T(8,128)(2,1)}), bf16[4,32,16,100]{3,2,0,1:T(8,128)(2,1)S(1)}, u32[]{:S(2)}, u32[]{:S(2)}) async-start(bf16[4,32,16,100]{3,2,0,1:T(8,128)(2,1)} %copy.30), calls=%async_computation | async-start | bytes 1048576 | tf_op jit(solution)/shard_map/all_to_all | solution.py:49
  42.1 22.3 %all-to-all-start.1 = ((bf16[4,32,16,100]{3,2,0,1:T(8,128)(2,1)}), bf16[4,32,16,100]{3,2,0,1:T(8,128)(2,1)S(1)}, u32[]{:S(2)}, u32[]{:S(2)}) async-start(bf16[4,32,16,100]{3,2,0,1:T(8,128)(2,1)} %copy.35), calls=%async_computation.1 | async-start | bytes 1048576 | tf_op jit(solution)/shard_map/all_to_all | solution.py:49
  46.6 178.9 %reduce-scatter.4.cloned.1.call-start = ((), (), s32[]{:S(2)}) async-start(), calls=%async_computation.3 | async-start | bytes 905216
Sparse Core Ops, SparseCore 0:
  66.3 159.2 reduce-scatter.3
where the time goes:
time: 290 us
  blocking collectives  121 us (42%)
  waiting for transfers between devices  110 us (38%)
  starting transfers between devices  15.6 us (5%)
  between operations  14.2 us (5%)
  other arithmetic  14 us (5%)
  local copies, waits for them, and re-layouts  13.2 us (5%)
    unnamed x2, waiting for transfers between devices  78.3 us
    all_gather x1, blocking collectives, local(): lax.all_gather(factor, 'grp', axis=0, tiled=True)  43 us
    unnamed x1, blocking collectives  42.8 us
    all_gather x1, blocking collectives, local(): lax.all_gather(mean_vec, 'grp', axis=0, tiled=True)  35.3 us
    all_to_all x2, waiting for transfers between devices, local(): lax.all_to_all(shaped, 'pos', split_axis=1, concat_axis=0, tiled=True)  31.6 us
    all_to_all x2, starting transfers between devices, local(): lax.all_to_all(shaped, 'pos', split_axis=1, concat_axis=0, tiled=True)  15.5 us
    another operation x3, other arithmetic, factorize(): return (jnp.linalg.cholesky(covariance), mean_vec)  9.91 us
  transfers between devices with their start and end apart: 3, of which 3 were waited for; matrix products, arithmetic and copies ran while one was open for 2% of the time, Pallas kernels for 0%

commit v1 on v0

v1 whole, which is shorter than its diff:
```python
import jax
import jax.numpy as jnp
from jax import lax
from jax.experimental import pallas as pl
from jax.experimental.pallas import tpu as pltpu
from jax.sharding import PartitionSpec as P

RIDGE = 0.01
LANES = 128
NX, NY, NZ = 4, 8, 8
GROUP = 32
SHARE = 16
ROWS = 104


def kernel(image_total, idx_ref, feat_ref, factor_ref, mean_ref,
           idx_pad, feat, wide, sbuf, rbuf, pbuf, r2buf, lbuf, r3buf,
           load_sem, send1, recv1, send2, recv2, send3, recv3):
    batches, imgs, width, positions = feat_ref.shape
    images = batches * imgs
    keep = idx_ref.shape[1]
    grp = lax.axis_index("grp")
    pos = lax.axis_index("pos")
    y, x_hi = grp // 2, grp % 2
    x_lo, z, core = pos // (2 * NZ), (pos // 2) % NZ, pos % 2
    x = 2 * x_hi + x_lo
    y_hi, y_lo = y // 2, y % 2
    z_hi, z_lo = z // 2, z % 2

    def device(xx, yy, zz, cc):
        return {"grp": yy * 2 + xx // 2, "pos": ((xx % 2) * NZ + zz) * 2 + cc}

    def partner1(t):
        xx = (x + t // 8) % 4
        zl = (z_lo + (t // 4) % 2) % 2
        yl = (y_lo + (t // 2) % 2) % 2
        cc = (core + t % 2) % 2
        return ((xx * 2 + zl) * 2 + yl) * 2 + cc, device(xx, 2 * y_hi + yl, 2 * z_hi + zl, cc)

    def partner2(t):
        q = (z_hi * 4 + y_hi + t) % 16
        return q, device(x, 2 * (q % 4) + y_lo, 2 * (q // 4) + z_lo, core)

    def partner3(t):
        o = (own + t) % 16
        xh, yl, yh = o // 8, (o // 4) % 2, o % 4
        return o, device(2 * xh + x_lo, 2 * yh + yl, z, core)

    me = ((x * 2 + z_lo) * 2 + y_lo) * 2 + core
    mine = z_hi * 4 + y_hi
    own = x_hi * 8 + y_lo * 4 + y_hi

    copies = []
    for b in range(batches):
        for i in range(imgs):
            k = b * imgs + i
            c = pltpu.make_async_copy(feat_ref.at[b, i], feat.at[k], load_sem.at[k])
            c.start()
            copies.append(c)

    barrier = pltpu.get_barrier_semaphore()

    def greet(partner):
        def body(t, carry):
            pl.semaphore_signal(barrier, inc=1, device_id=partner(t)[1], device_id_type=pl.DeviceIdType.MESH)
            return carry
        return body

    lax.fori_loop(1, GROUP, greet(partner1), 0)
    lax.fori_loop(1, 16, greet(partner2), 0)
    lax.fori_loop(1, 16, greet(partner3), 0)

    idx_pad[...] = jnp.full(idx_pad.shape, -1, jnp.int32)
    idx_pad[0:1, 0:keep] = idx_ref[...]
    selector = jnp.where(
        lax.broadcasted_iota(jnp.int32, (4 * LANES, LANES), 0) == idx_pad[0:1, :], 1.0, 0.0
    ).T[:, :width].astype(jnp.bfloat16)
    for k in range(images):
        copies[k].wait()
        picked = jnp.dot(selector, feat[k], preferred_element_type=jnp.float32)
        wide[pl.ds(k, positions, stride=images), :] = picked.T
    chunk = 4 * images
    ones_lane = lax.broadcasted_iota(jnp.int32, (chunk, LANES), 1) == keep
    for d in range(GROUP):
        xx, zl, yl, cc = d // 8, (d // 4) % 2, (d // 2) % 2, d % 2
        for zh in range(4):
            first = 16 * (((xx % 2) * NZ + 2 * zh + zl) * 2 + cc) + 8 * (xx // 2) + 4 * yl
            piece = wide[first * images:first * images + chunk, :]
            sbuf[d, zh * chunk:(zh + 1) * chunk, :] = jnp.where(ones_lane, 1.0, piece).astype(jnp.bfloat16)

    pl.semaphore_wait(barrier, GROUP - 1 + 15 + 15)

    def copy1(t):
        d, dev = partner1(t)
        return pltpu.make_async_remote_copy(
            src_ref=sbuf.at[d], dst_ref=rbuf.at[me], send_sem=send1.at[t], recv_sem=recv1.at[me],
            device_id=dev, device_id_type=pl.DeviceIdType.MESH)

    def got1(t):
        s, dev = partner1(t)
        return pltpu.make_async_remote_copy(
            src_ref=sbuf.at[s], dst_ref=rbuf.at[s], send_sem=send1.at[t], recv_sem=recv1.at[s],
            device_id=dev, device_id_type=pl.DeviceIdType.MESH)

    def loop(lo, hi, act):
        def body(t, carry):
            act(t)
            return carry
        lax.fori_loop(lo, hi, body, 0)

    loop(1, GROUP, lambda t: copy1(t).start())
    rbuf[me] = sbuf[me]
    loop(1, GROUP, lambda t: got1(t).wait_recv())

    half = (lax.broadcasted_iota(jnp.int32, (16, LANES), 0) < images).astype(jnp.float32)
    even = half.astype(jnp.bfloat16)
    odd = (1.0 - half).astype(jnp.bfloat16)

    def pair(j, carry):
        tile = rbuf[:, pl.ds(pl.multiple_of(16 * j, 16), 16), :]
        flat = tile.reshape(GROUP * 16, LANES)
        rhs = jnp.concatenate(
            [(tile * even[None]).reshape(GROUP * 16, LANES), (tile * odd[None]).reshape(GROUP * 16, LANES)], axis=1)
        both = lax.dot_general(flat, rhs, (((0,), (0,)), ((), ())), preferred_element_type=jnp.float32)
        pbuf[2 * j] = both[:ROWS, :LANES]
        pbuf[2 * j + 1] = both[:ROWS, LANES:]
        return carry

    lax.fori_loop(0, SHARE // 2, pair, 0)

    def copy2(t):
        q, dev = partner2(t)
        return pltpu.make_async_remote_copy(
            src_ref=pbuf.at[q], dst_ref=r2buf.at[mine], send_sem=send2.at[t], recv_sem=recv2.at[mine],
            device_id=dev, device_id_type=pl.DeviceIdType.MESH)

    def got2(t):
        s, dev = partner2(t)
        return pltpu.make_async_remote_copy(
            src_ref=pbuf.at[s], dst_ref=r2buf.at[s], send_sem=send2.at[t], recv_sem=recv2.at[s],
            device_id=dev, device_id_type=pl.DeviceIdType.MESH)

    loop(1, 16, lambda t: copy2(t).start())
    r2buf[mine] = pbuf[mine]
    loop(1, 16, lambda t: got2(t).wait_recv())
    total = jnp.sum(r2buf[...], axis=0)

    row = lax.broadcasted_iota(jnp.int32, (ROWS, LANES), 0)
    lane = lax.broadcasted_iota(jnp.int32, (ROWS, LANES), 1)
    mean_row = total[keep:keep + 1, :] / image_total
    mean_col = total[:, keep:keep + 1] / image_total
    cov = (total - (image_total * mean_col) * mean_row) / (image_total - 1)
    cov = cov + jnp.where(row == lane, RIDGE, 0.0)
    cov = jnp.where((row < keep) & (lane < keep), cov, jnp.where(row == lane, 1.0, 0.0))
    blocks = [cov[8 * i:8 * i + 8, :] for i in range(ROWS // 8)]
    sub = lax.broadcasted_iota(jnp.int32, (8, LANES), 0)

    def spread_row(v, k):
        return jnp.broadcast_to(v[k:k + 1, :], (8, LANES))

    upper = []
    count = ROWS // 8
    for j in range(count):
        cols = [[jnp.broadcast_to(blocks[i][:, 8 * j + k:8 * j + k + 1], (8, LANES)) for k in range(8)]
                for i in range(j, count)]
        root = jnp.zeros((8, LANES), jnp.float32)
        for k in range(8):
            pivot = spread_row(cols[0][k], k)
            inv = 1.0 / pivot
            root = jnp.where(sub == k, lax.rsqrt(pivot), root)
            main_row = spread_row(blocks[j], k) * inv
            col_rows = [spread_row(cols[0][m], k) * inv for m in range(k + 1, 8)]
            for i in range(j, count):
                left = cols[i - j][k]
                if i == j:
                    left = jnp.where(sub > k, left, 0.0)
                blocks[i] = blocks[i] - left * main_row
                for m in range(k + 1, 8):
                    cols[i - j][m] = cols[i - j][m] - left * col_rows[m - k - 1]
        upper.append(blocks[j] * root)
    full = jnp.concatenate(upper + [jnp.zeros((LANES - ROWS, LANES), jnp.float32)], axis=0)
    row128 = lax.broadcasted_iota(jnp.int32, (LANES, LANES), 0)
    lane128 = lax.broadcasted_iota(jnp.int32, (LANES, LANES), 1)
    full = jnp.where(lane128 >= row128, full, 0.0)
    lower = full.T
    lower = jnp.where(row128 < keep, lower, jnp.where(row128 == keep, mean_row, 0.0))
    lbuf[...] = lower[:ROWS, :]

    def copy3(t):
        o, dev = partner3(t)
        return pltpu.make_async_remote_copy(
            src_ref=lbuf, dst_ref=r3buf.at[own], send_sem=send3.at[t], recv_sem=recv3.at[own],
            device_id=dev, device_id_type=pl.DeviceIdType.MESH)

    def got3(t):
        s, dev = partner3(t)
        return pltpu.make_async_remote_copy(
            src_ref=lbuf, dst_ref=r3buf.at[s], send_sem=send3.at[t], recv_sem=recv3.at[s],
            device_id=dev, device_id_type=pl.DeviceIdType.MESH)

    loop(1, 16, lambda t: copy3(t).start())
    r3buf[own] = lbuf[...]
    loop(1, 16, lambda t: got3(t).wait_recv())
    for o in range(16):
        factor_ref[:, o, :] = r3buf[o, :keep, :keep]
        mean_ref[o:o + 1, :] = r3buf[o, keep:keep + 1, :keep]

    loop(1, GROUP, lambda t: copy1(t).wait_send())
    loop(1, 16, lambda t: copy2(t).wait_send())
    loop(1, 16, lambda t: copy3(t).wait_send())


def local(features, channel_index):
    batches, imgs, positions, width = features.shape
    keep = channel_index.shape[0]
    images = batches * imgs
    image_total = images * lax.axis_size("pos") * lax.axis_size("grp")
    owned = positions // lax.axis_size("pos")
    f32, bf16 = jnp.float32, jnp.bfloat16
    vmem = pl.BlockSpec(memory_space=pltpu.VMEM)
    factor, mean_vec = pl.pallas_call(
        lambda *refs: kernel(image_total, *refs),
        out_shape=(jax.ShapeDtypeStruct((keep, owned, keep), f32), jax.ShapeDtypeStruct((owned, keep), f32)),
        in_specs=[vmem, pl.BlockSpec(memory_space=pl.ANY)],
        out_specs=(vmem, vmem),
        scratch_shapes=[
            pltpu.VMEM((8, LANES), jnp.int32),
            pltpu.VMEM((images, width, positions), bf16),
            pltpu.VMEM((images * positions, LANES), f32),
            pltpu.VMEM((GROUP, SHARE * images, LANES), bf16),
            pltpu.VMEM((GROUP, SHARE * images, LANES), bf16),
            pltpu.VMEM((SHARE, ROWS, LANES), f32),
            pltpu.VMEM((SHARE, ROWS, LANES), f32),
            pltpu.VMEM((ROWS, LANES), f32),
            pltpu.VMEM((SHARE, ROWS, LANES), f32),
            pltpu.SemaphoreType.DMA((images,)),
            pltpu.SemaphoreType.DMA((GROUP,)),
            pltpu.SemaphoreType.DMA((GROUP,)),
            pltpu.SemaphoreType.DMA((16,)),
            pltpu.SemaphoreType.DMA((16,)),
            pltpu.SemaphoreType.DMA((16,)),
            pltpu.SemaphoreType.DMA((16,)),
        ],
        compiler_params=pltpu.CompilerParams(
            collective_id=0, has_side_effects=True, vmem_limit_bytes=60 * 1024 * 1024),
        name="gaussian_stats",
    )(channel_index.reshape(1, keep), jnp.swapaxes(features, 2, 3))
    return jnp.swapaxes(factor, 0, 1), mean_vec


def solution(mesh):
    return jax.shard_map(
        local,
        mesh=mesh,
        in_specs=(P(None, ("grp", "pos"), None, None), P()),
        out_specs=(P("pos", None, None), P("pos", None)),
        check_vma=False,
    )
```

time: 290 us -> 94.7 us (0.33)
  the two profiles are of different devices: /device:TPU:64 before, /device:TPU:1 now
where the time goes in v1:
time: 94.7 us; the launch traced here: 94.5 us
  Pallas kernels  90.4 us (95%)
  local copies, waits for them, and re-layouts  3.38 us (4%)
    pallas_call x1, Pallas kernels, local(): pl.pallas_call(lambda *refs: kernel(image_total, *refs), out_shape=(jax.S...  90.4 us
    unnamed x2, local copies, waits for them, and re-layouts  3.38 us

profile of v1, /device:TPU:1, one launch (start us, length us, event | category | flops | bytes accessed | tf_op | source)
XLA Modules:
  0.0 94.5 jit_solution(3832741946158331595)
XLA Ops:
  0.6 90.4 %gaussian_stats.1 = (f32[100,16,100]{2,1,0:T(8,128)}, f32[16,100]{1,0:T(8,128)}) custom-call(s32[1,100]{1,0:T(1,128)} %bitcast.5, bf16[2,4,448,512]{3,2,1,0:T(8,128)(2,1)} %bitcast.3), custom_call_target="tpu_custom_call" | custom-call | tf_op jit(solution)/shard_map/gaussian_stats/pallas_call | solution.py:221
  91.1 2.1 %copy.6 = f32[16,100,100]{2,0,1:T(8,128)} copy(f32[16,100,100]{2,0,1:T(8,128)} %bitcast.4) | data formatting | bytes 1280000
  93.2 1.3 %copy.7 = f32[16,100]{1,0:T(8,128)} copy(f32[16,100]{1,0:T(8,128)} %get-tuple-element.9) | data formatting | bytes 12800

commit v2 on v1

--- a/solution.py
+++ b/solution.py
@@ -11,6 +11,35 @@
 GROUP = 32
 SHARE = 16
 ROWS = 104
+HEAD, PACK = 56, 48
+
+
+def lanes_of(rows):
+    return lax.broadcasted_iota(jnp.int32, (rows, LANES), 1)
+
+
+def rows_of(rows):
+    return lax.broadcasted_iota(jnp.int32, (rows, LANES), 0)
+
+
+def pack(low, up):
+    row, lane = rows_of(PACK), lanes_of(PACK)
+    corner = pltpu.roll(up[PACK:HEAD, :], 116 - PACK, 1)
+    lane8 = lanes_of(8)
+    out = jnp.where(lane <= HEAD + row, low[HEAD:ROWS, :], pltpu.roll(up[:PACK, :], HEAD + 1, 1))
+    first = jnp.where((lane8 >= 116) & (lane8 < 124), corner, out[:8, :])
+    return jnp.concatenate([first, out[8:, :]], axis=0)
+
+
+def unpack_head(packed):
+    head = jnp.concatenate(
+        [pltpu.roll(packed, LANES - HEAD - 1, 1), pltpu.roll(packed[:8, :], LANES - 116 + PACK, 1)], axis=0)
+    lane = lanes_of(HEAD)
+    return jnp.where((lane >= rows_of(HEAD)) & (lane < HEAD), head, 0.0)
+
+
+def unpack_tail(packed):
+    return jnp.where(lanes_of(PACK) <= HEAD + rows_of(PACK), packed, 0.0)
 
 
 def kernel(image_total, idx_ref, feat_ref, factor_ref, mean_ref,
@@ -122,8 +151,8 @@
         rhs = jnp.concatenate(
             [(tile * even[None]).reshape(GROUP * 16, LANES), (tile * odd[None]).reshape(GROUP * 16, LANES)], axis=1)
         both = lax.dot_general(flat, rhs, (((0,), (0,)), ((), ())), preferred_element_type=jnp.float32)
-        pbuf[2 * j] = both[:ROWS, :LANES]
-        pbuf[2 * j + 1] = both[:ROWS, LANES:]
+        pbuf[2 * j] = pack(both[:, :LANES], both[:, :LANES])
+        pbuf[2 * j + 1] = pack(both[:, LANES:], both[:, LANES:])
         return carry
 
     lax.fori_loop(0, SHARE // 2, pair, 0)
@@ -143,7 +172,11 @@
     loop(1, 16, lambda t: copy2(t).start())
     r2buf[mine] = pbuf[mine]
     loop(1, 16, lambda t: got2(t).wait_recv())
-    total = jnp.sum(r2buf[...], axis=0)
+    packed = jnp.sum(r2buf[...], axis=0)
+    half_total = jnp.concatenate(
+        [unpack_head(packed), unpack_tail(packed), jnp.zeros((LANES - ROWS, LANES), jnp.float32)], axis=0)
+    row128, lane128 = rows_of(LANES), lanes_of(LANES)
+    total = (half_total + jnp.where(row128 == lane128, 0.0, half_total.T))[:ROWS, :]
 
     row = lax.broadcasted_iota(jnp.int32, (ROWS, LANES), 0)
     lane = lax.broadcasted_iota(jnp.int32, (ROWS, LANES), 1)
@@ -179,12 +212,13 @@
                     cols[i - j][m] = cols[i - j][m] - left * col_rows[m - k - 1]
         upper.append(blocks[j] * root)
     full = jnp.concatenate(upper + [jnp.zeros((LANES - ROWS, LANES), jnp.float32)], axis=0)
-    row128 = lax.broadcasted_iota(jnp.int32, (LANES, LANES), 0)
-    lane128 = lax.broadcasted_iota(jnp.int32, (LANES, LANES), 1)
     full = jnp.where(lane128 >= row128, full, 0.0)
     lower = full.T
-    lower = jnp.where(row128 < keep, lower, jnp.where(row128 == keep, mean_row, 0.0))
-    lbuf[...] = lower[:ROWS, :]
+    out = pack(lower, full)
+    lane48 = lanes_of(PACK)
+    means = jnp.where(lane48 == 113, mean_col[:PACK], mean_col[PACK:2 * PACK])
+    lbuf[...] = jnp.where((lane48 == 113) | (lane48 == 114), means, out)
+    lbuf[:8, :] = jnp.where(lanes_of(8) == 115, mean_col[2 * PACK:], lbuf[:8, :])
 
     def copy3(t):
         o, dev = partner3(t)
@@ -201,9 +235,26 @@
     loop(1, 16, lambda t: copy3(t).start())
     r3buf[own] = lbuf[...]
     loop(1, 16, lambda t: got3(t).wait_recv())
-    for o in range(16):
-        factor_ref[:, o, :] = r3buf[o, :keep, :keep]
-        mean_ref[o:o + 1, :] = r3buf[o, keep:keep + 1, :keep]
+    for o in range(0, 16, 2):
+        turned = []
+        for i in range(2):
+            mine3 = r3buf[o + i]
+            turn = pltpu.roll(mine3, LANES - HEAD - 1, 1)
+            extra = pltpu.roll(mine3[:8, :], LANES - 116 + PACK, 1)
+            lane = lanes_of(PACK)
+            turn = jnp.where((lane >= rows_of(PACK)) & (lane < HEAD + 3), turn, 0.0)
+            lane8 = lanes_of(8)
+            extra = jnp.where((lane8 >= PACK + rows_of(8)) & (lane8 < HEAD), extra, 0.0)
+            turned.append(jnp.concatenate([turn, extra, jnp.zeros((8, LANES), jnp.float32)], axis=0))
+        both = (turned[0] + pltpu.roll(turned[1], 64, 1)).T
+        for i in range(2):
+            head = both[64 * i:64 * i + 64, :]
+            factor_ref[0:HEAD, o + i, 0:64] = head[:HEAD, :]
+            factor_ref[0:HEAD, o + i, 64:keep] = jnp.zeros((HEAD, keep - 64), jnp.float32)
+            factor_ref[HEAD:keep, o + i, :] = unpack_tail(r3buf[o + i])[:keep - HEAD, :keep]
+            mean_ref[o + i:o + i + 1, 0:PACK] = head[HEAD:HEAD + 1, :PACK]
+            mean_ref[o + i:o + i + 1, PACK:2 * PACK] = head[HEAD + 1:HEAD + 2, :PACK]
+            mean_ref[o + i:o + i + 1, 2 * PACK:keep] = head[HEAD + 2:HEAD + 3, :keep - 2 * PACK]
 
     loop(1, GROUP, lambda t: copy1(t).wait_send())
     loop(1, 16, lambda t: copy2(t).wait_send())
@@ -229,10 +280,10 @@
             pltpu.VMEM((images * positions, LANES), f32),
             pltpu.VMEM((GROUP, SHARE * images, LANES), bf16),
             pltpu.VMEM((GROUP, SHARE * images, LANES), bf16),
-            pltpu.VMEM((SHARE, ROWS, LANES), f32),
-            pltpu.VMEM((SHARE, ROWS, LANES), f32),
-            pltpu.VMEM((ROWS, LANES), f32),
-            pltpu.VMEM((SHARE, ROWS, LANES), f32),
+            pltpu.VMEM((SHARE, PACK, LANES), f32),
+            pltpu.VMEM((SHARE, PACK, LANES), f32),
+            pltpu.VMEM((PACK, LANES), f32),
+            pltpu.VMEM((SHARE, PACK, LANES), f32),
             pltpu.SemaphoreType.DMA((images,)),
             pltpu.SemaphoreType.DMA((GROUP,)),
             pltpu.SemaphoreType.DMA((GROUP,)),

time: 94.7 us -> 71.6 us (0.76)
  Pallas kernels: 90.4 us -> 66.4 us
    pallas_call x1, Pallas kernels: 90.4 us -> 66.4 us  [local(): pl.pallas_call(lambda *refs: kernel(image_total, *refs), out_shape=(jax.S...]
where the time goes in v2:
time: 71.6 us; the launch traced here: 70.4 us
  Pallas kernels  66.4 us (93%)
  local copies, waits for them, and re-layouts  3.38 us (5%)
    pallas_call x1, Pallas kernels, local(): pl.pallas_call(lambda *refs: kernel(image_total, *refs), out_shape=(jax.S...  66.4 us
    unnamed x2, local copies, waits for them, and re-layouts  3.38 us

profile of v2, /device:TPU:1, one launch (start us, length us, event | category | flops | bytes accessed | tf_op | source)
XLA Modules:
  0.0 70.4 jit_solution(2524048466101379276)
XLA Ops:
  0.6 66.4 %gaussian_stats.1 = (f32[100,16,100]{2,1,0:T(8,128)}, f32[16,100]{1,0:T(8,128)}) custom-call(s32[1,100]{1,0:T(1,128)} %bitcast.5, bf16[2,4,448,512]{3,2,1,0:T(8,128)(2,1)} %bitcast.3), custom_call_target="tpu_custom_call" | custom-call | tf_op jit(solution)/shard_map/gaussian_stats/pallas_call | solution.py:272
  67.1 2.1 %copy.6 = f32[16,100,100]{2,0,1:T(8,128)} copy(f32[16,100,100]{2,0,1:T(8,128)} %bitcast.4) | data formatting | bytes 1280000
  69.2 1.3 %copy.7 = f32[16,100]{1,0:T(8,128)} copy(f32[16,100]{1,0:T(8,128)} %get-tuple-element.9) | data formatting | bytes 12800

commit v3 on v2

--- a/solution.py
+++ b/solution.py
@@ -42,9 +42,18 @@
     return jnp.where(lanes_of(PACK) <= HEAD + rows_of(PACK), packed, 0.0)
 
 
-def kernel(image_total, idx_ref, feat_ref, factor_ref, mean_ref,
-           idx_pad, feat, wide, sbuf, rbuf, pbuf, r2buf, lbuf, r3buf,
-           load_sem, send1, recv1, send2, recv2, send3, recv3):
+def ring(d, n):
+    return min(d, n - d)
+
+
+ORDER1 = sorted(range(1, GROUP), key=lambda t: -(ring(t // 8, 4) + (t // 4) % 2 + (t // 2) % 2))
+ORDER3 = sorted(range(1, 8), key=lambda t: -ring(t, 8))
+ORDER2 = sorted(range(1, 16), key=lambda t: -2 * (ring(t // 4, 4) + ring(t % 4, 4)))
+
+
+def kernel(image_total, idx_ref, feat_ref, r3buf,
+           idx, idx_pad, feat, wide, sbuf, rbuf, pbuf, r2buf, lbuf,
+           idx_sem, load_sem, send1, recv1, send2, recv2, send3, recv3):
     batches, imgs, width, positions = feat_ref.shape
     images = batches * imgs
     keep = idx_ref.shape[1]
@@ -67,18 +76,24 @@
         return ((xx * 2 + zl) * 2 + yl) * 2 + cc, device(xx, 2 * y_hi + yl, 2 * z_hi + zl, cc)
 
     def partner2(t):
-        q = (z_hi * 4 + y_hi + t) % 16
+        q = ((z_hi + t // 4) % 4) * 4 + (y_hi + t % 4) % 4
         return q, device(x, 2 * (q % 4) + y_lo, 2 * (q // 4) + z_lo, core)
 
+    def place(xh, yy):
+        return xh * 8 + (yy % 2) * 4 + yy // 2
+
     def partner3(t):
-        o = (own + t) % 16
-        xh, yl, yh = o // 8, (o // 4) % 2, o % 4
-        return o, device(2 * xh + x_lo, 2 * yh + yl, z, core)
+        yy = (y + t) % 8
+        return place(x_hi, yy), device(x, yy, z, core)
+
+    across = device((x + 2) % 4, y, z, core)
 
     me = ((x * 2 + z_lo) * 2 + y_lo) * 2 + core
     mine = z_hi * 4 + y_hi
     own = x_hi * 8 + y_lo * 4 + y_hi
 
+    idx_copy = pltpu.make_async_copy(idx_ref, idx, idx_sem)
+    idx_copy.start()
     copies = []
     for b in range(batches):
         for i in range(imgs):
@@ -89,18 +104,17 @@
 
     barrier = pltpu.get_barrier_semaphore()
 
-    def greet(partner):
-        def body(t, carry):
-            pl.semaphore_signal(barrier, inc=1, device_id=partner(t)[1], device_id_type=pl.DeviceIdType.MESH)
-            return carry
-        return body
-
-    lax.fori_loop(1, GROUP, greet(partner1), 0)
-    lax.fori_loop(1, 16, greet(partner2), 0)
-    lax.fori_loop(1, 16, greet(partner3), 0)
+    greetings = [partner2(t)[1] for t in ORDER2] + [partner1(t)[1] for t in ORDER1]
+
+    def greet(devices):
+        for dev in devices:
+            pl.semaphore_signal(barrier, inc=1, device_id=dev, device_id_type=pl.DeviceIdType.MESH)
+
+    greet(greetings)
 
     idx_pad[...] = jnp.full(idx_pad.shape, -1, jnp.int32)
-    idx_pad[0:1, 0:keep] = idx_ref[...]
+    idx_copy.wait()
+    idx_pad[0:1, 0:keep] = idx[...]
     selector = jnp.where(
         lax.broadcasted_iota(jnp.int32, (4 * LANES, LANES), 0) == idx_pad[0:1, :], 1.0, 0.0
     ).T[:, :width].astype(jnp.bfloat16)
@@ -117,7 +131,7 @@
             piece = wide[first * images:first * images + chunk, :]
             sbuf[d, zh * chunk:(zh + 1) * chunk, :] = jnp.where(ones_lane, 1.0, piece).astype(jnp.bfloat16)
 
-    pl.semaphore_wait(barrier, GROUP - 1 + 15 + 15)
+    pl.semaphore_wait(barrier, GROUP - 1 + 15)
 
     def copy1(t):
         d, dev = partner1(t)
@@ -137,7 +151,8 @@
             return carry
         lax.fori_loop(lo, hi, body, 0)
 
-    loop(1, GROUP, lambda t: copy1(t).start())
+    for t in ORDER1:
+        copy1(t).start()
     rbuf[me] = sbuf[me]
     loop(1, GROUP, lambda t: got1(t).wait_recv())
 
@@ -145,7 +160,15 @@
     even = half.astype(jnp.bfloat16)
     odd = (1.0 - half).astype(jnp.bfloat16)
 
-    def pair(j, carry):
+    def copy2(q, n):
+        dev = device(x, 2 * (q % 4) + y_lo, 2 * (q // 4) + z_lo, core)
+        return pltpu.make_async_remote_copy(
+            src_ref=pbuf.at[q], dst_ref=r2buf.at[mine], send_sem=send2.at[n], recv_sem=recv2.at[mine],
+            device_id=dev, device_id_type=pl.DeviceIdType.MESH)
+
+    sent2 = []
+    for dz, dy in ((2, 1), (2, 0), (1, 1), (3, 1), (1, 0), (3, 0), (0, 1), (0, 0)):
+        j = ((z_hi + dz) % 4) * 2 + (y_hi // 2 + dy) % 2
         tile = rbuf[:, pl.ds(pl.multiple_of(16 * j, 16), 16), :]
         flat = tile.reshape(GROUP * 16, LANES)
         rhs = jnp.concatenate(
@@ -153,15 +176,10 @@
         both = lax.dot_general(flat, rhs, (((0,), (0,)), ((), ())), preferred_element_type=jnp.float32)
         pbuf[2 * j] = pack(both[:, :LANES], both[:, :LANES])
         pbuf[2 * j + 1] = pack(both[:, LANES:], both[:, LANES:])
-        return carry
-
-    lax.fori_loop(0, SHARE // 2, pair, 0)
-
-    def copy2(t):
-        q, dev = partner2(t)
-        return pltpu.make_async_remote_copy(
-            src_ref=pbuf.at[q], dst_ref=r2buf.at[mine], send_sem=send2.at[t], recv_sem=recv2.at[mine],
-            device_id=dev, device_id_type=pl.DeviceIdType.MESH)
+        for q in ([2 * j, 2 * j + 1] if dz or dy else [2 * j + 1 - y_hi % 2]):
+            copy = copy2(q, len(sent2))
+            copy.start()
+            sent2.append(copy)
 
     def got2(t):
         s, dev = partner2(t)
@@ -169,7 +187,6 @@
             src_ref=pbuf.at[s], dst_ref=r2buf.at[s], send_sem=send2.at[t], recv_sem=recv2.at[s],
             device_id=dev, device_id_type=pl.DeviceIdType.MESH)
 
-    loop(1, 16, lambda t: copy2(t).start())
     r2buf[mine] = pbuf[mine]
     loop(1, 16, lambda t: got2(t).wait_recv())
     packed = jnp.sum(r2buf[...], axis=0)
@@ -220,25 +237,48 @@
     lbuf[...] = jnp.where((lane48 == 113) | (lane48 == 114), means, out)
     lbuf[:8, :] = jnp.where(lanes_of(8) == 115, mean_col[2 * PACK:], lbuf[:8, :])
 
-    def copy3(t):
-        o, dev = partner3(t)
-        return pltpu.make_async_remote_copy(
-            src_ref=lbuf, dst_ref=r3buf.at[own], send_sem=send3.at[t], recv_sem=recv3.at[own],
-            device_id=dev, device_id_type=pl.DeviceIdType.MESH)
-
-    def got3(t):
-        s, dev = partner3(t)
-        return pltpu.make_async_remote_copy(
-            src_ref=lbuf, dst_ref=r3buf.at[s], send_sem=send3.at[t], recv_sem=recv3.at[s],
-            device_id=dev, device_id_type=pl.DeviceIdType.MESH)
-
-    loop(1, 16, lambda t: copy3(t).start())
+    def copy3(src, o, dev, n):
+        return pltpu.make_async_remote_copy(
+            src_ref=src, dst_ref=r3buf.at[o], send_sem=send3.at[n], recv_sem=recv3.at[o],
+            device_id=dev, device_id_type=pl.DeviceIdType.MESH)
+
+    near, far = (6, 2, 7, 1), (4, 3, 5)
+
+    def beyond(t):
+        return device((x + 2) % 4, (y + t) % 8, z, core)
+
+    sent3 = [copy3(lbuf, own, partner3(t)[1], t) for t in far]
+    for t in near:
+        sent3.append(copy3(lbuf, own, beyond(t), 8 + t))
+        sent3.append(copy3(lbuf, own, partner3(t)[1], t))
+    sent3.append(copy3(lbuf, own, across, 0))
+    for copy in sent3:
+        copy.start()
     r3buf[own] = lbuf[...]
-    loop(1, 16, lambda t: got3(t).wait_recv())
+    for t in far:
+        o = partner3(t)[0]
+        copy3(lbuf, o, across, 8 + t).wait_recv()
+        copy = copy3(r3buf.at[o], o, across, 8 + t)
+        copy.start()
+        sent3.append(copy)
+    for t in near:
+        copy3(lbuf, partner3(t)[0], across, 8 + t).wait_recv()
+    for t in range(8):
+        copy3(lbuf, place((x_hi + 1) % 2, (y + t) % 8), across, 0).wait_recv()
+
+    loop(1, GROUP, lambda t: copy1(t).wait_send())
+    for copy in sent2:
+        copy.wait_send()
+    for copy in sent3:
+        copy.wait_send()
+
+
+def spread(packed_ref, factor_ref, mean_ref):
+    keep = mean_ref.shape[1]
     for o in range(0, 16, 2):
         turned = []
         for i in range(2):
-            mine3 = r3buf[o + i]
+            mine3 = packed_ref[o + i]
             turn = pltpu.roll(mine3, LANES - HEAD - 1, 1)
             extra = pltpu.roll(mine3[:8, :], LANES - 116 + PACK, 1)
             lane = lanes_of(PACK)
@@ -251,14 +291,10 @@
             head = both[64 * i:64 * i + 64, :]
             factor_ref[0:HEAD, o + i, 0:64] = head[:HEAD, :]
             factor_ref[0:HEAD, o + i, 64:keep] = jnp.zeros((HEAD, keep - 64), jnp.float32)
-            factor_ref[HEAD:keep, o + i, :] = unpack_tail(r3buf[o + i])[:keep - HEAD, :keep]
+            factor_ref[HEAD:keep, o + i, :] = unpack_tail(packed_ref[o + i])[:keep - HEAD, :keep]
             mean_ref[o + i:o + i + 1, 0:PACK] = head[HEAD:HEAD + 1, :PACK]
             mean_ref[o + i:o + i + 1, PACK:2 * PACK] = head[HEAD + 1:HEAD + 2, :PACK]
             mean_ref[o + i:o + i + 1, 2 * PACK:keep] = head[HEAD + 2:HEAD + 3, :keep - 2 * PACK]
-
-    loop(1, GROUP, lambda t: copy1(t).wait_send())
-    loop(1, 16, lambda t: copy2(t).wait_send())
-    loop(1, 16, lambda t: copy3(t).wait_send())
 
 
 def local(features, channel_index):
@@ -269,12 +305,13 @@
     owned = positions // lax.axis_size("pos")
     f32, bf16 = jnp.float32, jnp.bfloat16
     vmem = pl.BlockSpec(memory_space=pltpu.VMEM)
-    factor, mean_vec = pl.pallas_call(
+    packed = pl.pallas_call(
         lambda *refs: kernel(image_total, *refs),
-        out_shape=(jax.ShapeDtypeStruct((keep, owned, keep), f32), jax.ShapeDtypeStruct((owned, keep), f32)),
-        in_specs=[vmem, pl.BlockSpec(memory_space=pl.ANY)],
-        out_specs=(vmem, vmem),
+        out_shape=pltpu.VMEM((owned, PACK, LANES), f32),
+        in_specs=[pl.BlockSpec(memory_space=pl.ANY)] * 2,
+        out_specs=vmem,
         scratch_shapes=[
+            pltpu.VMEM((1, keep), jnp.int32),
             pltpu.VMEM((8, LANES), jnp.int32),
             pltpu.VMEM((images, width, positions), bf16),
             pltpu.VMEM((images * positions, LANES), f32),
@@ -283,7 +320,7 @@
             pltpu.VMEM((SHARE, PACK, LANES), f32),
             pltpu.VMEM((SHARE, PACK, LANES), f32),
             pltpu.VMEM((PACK, LANES), f32),
-            pltpu.VMEM((SHARE, PACK, LANES), f32),
+            pltpu.SemaphoreType.DMA,
             pltpu.SemaphoreType.DMA((images,)),
             pltpu.SemaphoreType.DMA((GROUP,)),
             pltpu.SemaphoreType.DMA((GROUP,)),
@@ -295,7 +332,15 @@
         compiler_params=pltpu.CompilerParams(
             collective_id=0, has_side_effects=True, vmem_limit_bytes=60 * 1024 * 1024),
         name="gaussian_stats",
-    )(channel_index.reshape(1, keep), jnp.swapaxes(features, 2, 3))
+    )(channel_index.reshape(1, keep), pltpu.with_memory_space_constraint(jnp.swapaxes(features, 2, 3), pltpu.HBM))
+    factor, mean_vec = pl.pallas_call(
+        spread,
+        out_shape=(jax.ShapeDtypeStruct((keep, owned, keep), f32), jax.ShapeDtypeStruct((owned, keep), f32)),
+        in_specs=[vmem],
+        out_specs=(vmem, vmem),
+        compiler_params=pltpu.CompilerParams(vmem_limit_bytes=16 * 1024 * 1024),
+        name="spread",
+    )(packed)
     return jnp.swapaxes(factor, 0, 1), mean_vec
 
 

time: 71.6 us -> 60.5 us (0.84); the launches traced: 70.4 us -> 60.3 us
  Pallas kernels: 66.4 us -> 59.7 us
  local copies, waits for them, and re-layouts: 3.38 us -> 0 us
    pallas_call x1 -> x2, Pallas kernels: 66.4 us -> 59.7 us  [the longest x1 57.4 us: local(): pl.pallas_call(lambda *refs: kernel(image_total, *refs), out_shape=pltpu....]
    unnamed x2 -> x0, local copies, waits for them, and re-layouts: 3.38 us -> none
where the time goes in v3:
time: 60.5 us; the launch traced here: 60.3 us
  Pallas kernels  59.7 us (99%)
  between operations  0.64 us (1%)
    pallas_call x1, Pallas kernels, local(): pl.pallas_call(lambda *refs: kernel(image_total, *refs), out_shape=pltpu....  57.4 us
    pallas_call x1, Pallas kernels, local(): pl.pallas_call(spread, out_shape=(jax.ShapeDtypeStruct((keep, owned, keep...  2.29 us

profile of v3, /device:TPU:1, one launch (start us, length us, event | category | flops | bytes accessed | tf_op | source)
XLA Modules:
  0.0 60.3 jit_solution(9882792324702331667)
XLA Ops:
  0.6 57.4 %gaussian_stats.1.packed_ref = f32[16,48,128]{2,1,0:T(8,128)S(1)} custom-call(s32[1,100]{1,0:T(1,128)} %bitcast.4, bf16[2,4,448,512]{3,2,1,0:T(8,128)(2,1)} %bitcast.3), custom_call_target="tpu_custom_call" | custom-call | tf_op jit(solution)/shard_map/gaussian_stats/pallas_call | solution.py:308
  58.0 2.3 %spread.1 = (f32[100,16,100]{2,1,0:T(8,128)}, f32[16,100]{1,0:T(8,128)}) custom-call(f32[16,48,128]{2,1,0:T(8,128)S(1)} %gaussian_stats.1.packed_ref), custom_call_target="tpu_custom_call" | custom-call | tf_op jit(solution)/shard_map/spread/pallas_call | solution.py:336

commit v4 on v3

--- a/solution.py
+++ b/solution.py
@@ -46,13 +46,14 @@
     return min(d, n - d)
 
 
-ORDER1 = sorted(range(1, GROUP), key=lambda t: -(ring(t // 8, 4) + (t // 4) % 2 + (t // 2) % 2))
+ORDER1 = [t for t in (8 * dx + 4 * dz + 2 * dy + dc for dz, dy in ((1, 1), (1, 0), (0, 1), (0, 0)) for dc in range(2)
+                      for dx in (2, 1, 3, 0)) if t]
 ORDER3 = sorted(range(1, 8), key=lambda t: -ring(t, 8))
 ORDER2 = sorted(range(1, 16), key=lambda t: -2 * (ring(t // 4, 4) + ring(t % 4, 4)))
 
 
-def kernel(image_total, idx_ref, feat_ref, r3buf,
-           idx, idx_pad, feat, wide, sbuf, rbuf, pbuf, r2buf, lbuf,
+def kernel(image_total, idx_ref, feat_ref, factor_ref, mean_ref,
+           idx, idx_pad, feat, wide, sbuf, rbuf, pbuf, r2buf, lbuf, r3buf,
            idx_sem, load_sem, send1, recv1, send2, recv2, send3, recv3):
     batches, imgs, width, positions = feat_ref.shape
     images = batches * imgs
@@ -261,24 +262,19 @@
         copy = copy3(r3buf.at[o], o, across, 8 + t)
         copy.start()
         sent3.append(copy)
-    for t in near:
-        copy3(lbuf, partner3(t)[0], across, 8 + t).wait_recv()
-    for t in range(8):
-        copy3(lbuf, place((x_hi + 1) % 2, (y + t) % 8), across, 0).wait_recv()
-
-    loop(1, GROUP, lambda t: copy1(t).wait_send())
-    for copy in sent2:
-        copy.wait_send()
-    for copy in sent3:
-        copy.wait_send()
-
-
-def spread(packed_ref, factor_ref, mean_ref):
-    keep = mean_ref.shape[1]
     for o in range(0, 16, 2):
+        for i in (o, o + 1):
+            ahead = (2 * (i % 4) + (i // 4) % 2 + 8 - y) % 8
+            here = jnp.where(i // 8 == x_hi, 1, 0)
+            known = jnp.where((ahead == 0) | ((ahead >= 3) & (ahead <= 5)), 1, 0) * here
+
+            @pl.when(known == 0)
+            def _():
+                copy3(lbuf, i, across, 0).wait_recv()
+
         turned = []
         for i in range(2):
-            mine3 = packed_ref[o + i]
+            mine3 = r3buf[o + i]
             turn = pltpu.roll(mine3, LANES - HEAD - 1, 1)
             extra = pltpu.roll(mine3[:8, :], LANES - 116 + PACK, 1)
             lane = lanes_of(PACK)
@@ -291,10 +287,25 @@
             head = both[64 * i:64 * i + 64, :]
             factor_ref[0:HEAD, o + i, 0:64] = head[:HEAD, :]
             factor_ref[0:HEAD, o + i, 64:keep] = jnp.zeros((HEAD, keep - 64), jnp.float32)
-            factor_ref[HEAD:keep, o + i, :] = unpack_tail(packed_ref[o + i])[:keep - HEAD, :keep]
+            factor_ref[HEAD:keep, o + i, :] = unpack_tail(r3buf[o + i])[:keep - HEAD, :keep]
             mean_ref[o + i:o + i + 1, 0:PACK] = head[HEAD:HEAD + 1, :PACK]
             mean_ref[o + i:o + i + 1, PACK:2 * PACK] = head[HEAD + 1:HEAD + 2, :PACK]
             mean_ref[o + i:o + i + 1, 2 * PACK:keep] = head[HEAD + 2:HEAD + 3, :keep - 2 * PACK]
+
+    loop(1, GROUP, lambda t: copy1(t).wait_send())
+    for copy in sent2:
+        copy.wait_send()
+    for copy in sent3:
+        copy.wait_send()
+
+
+def store(factor_in, mean_in, factor_ref, mean_ref, sems):
+    copies = [pltpu.make_async_copy(factor_in, factor_ref, sems.at[0]),
+              pltpu.make_async_copy(mean_in, mean_ref, sems.at[1])]
+    for copy in copies:
+        copy.start()
+    for copy in copies:
+        copy.wait()
 
 
 def local(features, channel_index):
@@ -305,11 +316,11 @@
     owned = positions // lax.axis_size("pos")
     f32, bf16 = jnp.float32, jnp.bfloat16
     vmem = pl.BlockSpec(memory_space=pltpu.VMEM)
-    packed = pl.pallas_call(
+    factor, mean_vec = pl.pallas_call(
         lambda *refs: kernel(image_total, *refs),
-        out_shape=pltpu.VMEM((owned, PACK, LANES), f32),
+        out_shape=(pltpu.VMEM((keep, owned, keep), f32), pltpu.VMEM((owned, keep), f32)),
         in_specs=[pl.BlockSpec(memory_space=pl.ANY)] * 2,
-        out_specs=vmem,
+        out_specs=(vmem, vmem),
         scratch_shapes=[
             pltpu.VMEM((1, keep), jnp.int32),
             pltpu.VMEM((8, LANES), jnp.int32),
@@ -320,6 +331,7 @@
             pltpu.VMEM((SHARE, PACK, LANES), f32),
             pltpu.VMEM((SHARE, PACK, LANES), f32),
             pltpu.VMEM((PACK, LANES), f32),
+            pltpu.VMEM((SHARE, PACK, LANES), f32),
             pltpu.SemaphoreType.DMA,
             pltpu.SemaphoreType.DMA((images,)),
             pltpu.SemaphoreType.DMA((GROUP,)),
@@ -334,13 +346,14 @@
         name="gaussian_stats",
     )(channel_index.reshape(1, keep), pltpu.with_memory_space_constraint(jnp.swapaxes(features, 2, 3), pltpu.HBM))
     factor, mean_vec = pl.pallas_call(
-        spread,
+        store,
         out_shape=(jax.ShapeDtypeStruct((keep, owned, keep), f32), jax.ShapeDtypeStruct((owned, keep), f32)),
-        in_specs=[vmem],
-        out_specs=(vmem, vmem),
+        in_specs=[vmem, vmem],
+        out_specs=(pl.BlockSpec(memory_space=pl.ANY), pl.BlockSpec(memory_space=pl.ANY)),
+        scratch_shapes=[pltpu.SemaphoreType.DMA((2,))],
         compiler_params=pltpu.CompilerParams(vmem_limit_bytes=16 * 1024 * 1024),
-        name="spread",
-    )(packed)
+        name="store",
+    )(factor, mean_vec)
     return jnp.swapaxes(factor, 0, 1), mean_vec
 
 

time: 60.5 us -> 60 us (level); the launches traced: 60.3 us -> 58.9 us
  Pallas kernels: 59.7 us -> 58.3 us
    pallas_call x2, Pallas kernels: 59.7 us -> 58.3 us  [the longest x1 57.4 us: local(): pl.pallas_call(lambda *refs: kernel(image_total, *refs), out_shape=(pltpu...]
where the time goes in v4:
time: 60 us; the launch traced here: 58.9 us
  Pallas kernels  58.3 us (97%)
  between operations  0.64 us (1%)
    pallas_call x1, Pallas kernels, local(): pl.pallas_call(lambda *refs: kernel(image_total, *refs), out_shape=(pltpu...  57.4 us

profile of v4, /device:TPU:1, one launch (start us, length us, event | category | flops | bytes accessed | tf_op | source)
XLA Modules:
  0.0 58.9 jit_solution(2834040568518161298)
XLA Ops:
  0.6 57.4 %gaussian_stats.1 = (f32[100,16,100]{2,1,0:T(8,128)S(1)}, f32[16,100]{1,0:T(8,128)S(1)}) custom-call(s32[1,100]{1,0:T(1,128)} %bitcast.4, bf16[2,4,448,512]{3,2,1,0:T(8,128)(2,1)} %bitcast.3), custom_call_target="tpu_custom_call" | custom-call | tf_op jit(solution)/shard_map/gaussian_stats/pallas_call | solution.py:319
  58.0 0.9 %store.1 = (f32[100,16,100]{2,1,0:T(8,128)}, f32[16,100]{1,0:T(8,128)}) custom-call(f32[100,16,100]{2,1,0:T(8,128)S(1)} %get-tuple-element.6.factor_in, f32[16,100]{1,0:T(8,128)S(1)} %get-tuple-element.7.mean_in), custom_call_target="tpu_custom_call" | custom-call | tf_op jit(solution)/shard_map/store/pallas_call | solution.py:348

commit v5 on v4

--- a/solution.py
+++ b/solution.py
@@ -287,7 +287,7 @@
             head = both[64 * i:64 * i + 64, :]
             factor_ref[0:HEAD, o + i, 0:64] = head[:HEAD, :]
             factor_ref[0:HEAD, o + i, 64:keep] = jnp.zeros((HEAD, keep - 64), jnp.float32)
-            factor_ref[HEAD:keep, o + i, :] = unpack_tail(r3buf[o + i])[:keep - HEAD, :keep]
+            factor_ref[HEAD:ROWS, o + i, :] = unpack_tail(r3buf[o + i])[:, :keep]
             mean_ref[o + i:o + i + 1, 0:PACK] = head[HEAD:HEAD + 1, :PACK]
             mean_ref[o + i:o + i + 1, PACK:2 * PACK] = head[HEAD + 1:HEAD + 2, :PACK]
             mean_ref[o + i:o + i + 1, 2 * PACK:keep] = head[HEAD + 2:HEAD + 3, :keep - 2 * PACK]
@@ -300,7 +300,7 @@
 
 
 def store(factor_in, mean_in, factor_ref, mean_ref, sems):
-    copies = [pltpu.make_async_copy(factor_in, factor_ref, sems.at[0]),
+    copies = [pltpu.make_async_copy(factor_in.at[pl.ds(0, factor_ref.shape[0])], factor_ref, sems.at[0]),
               pltpu.make_async_copy(mean_in, mean_ref, sems.at[1])]
     for copy in copies:
         copy.start()
@@ -318,14 +318,14 @@
     vmem = pl.BlockSpec(memory_space=pltpu.VMEM)
     factor, mean_vec = pl.pallas_call(
         lambda *refs: kernel(image_total, *refs),
-        out_shape=(pltpu.VMEM((keep, owned, keep), f32), pltpu.VMEM((owned, keep), f32)),
+        out_shape=(pltpu.VMEM((ROWS, owned, keep), f32), pltpu.VMEM((owned, keep), f32)),
         in_specs=[pl.BlockSpec(memory_space=pl.ANY)] * 2,
         out_specs=(vmem, vmem),
         scratch_shapes=[
             pltpu.VMEM((1, keep), jnp.int32),
             pltpu.VMEM((8, LANES), jnp.int32),
             pltpu.VMEM((images, width, positions), bf16),
-            pltpu.VMEM((images * positions, LANES), f32),
+            pltpu.VMEM((images * positions + 8, LANES), f32),
             pltpu.VMEM((GROUP, SHARE * images, LANES), bf16),
             pltpu.VMEM((GROUP, SHARE * images, LANES), bf16),
             pltpu.VMEM((SHARE, PACK, LANES), f32),

time: 60 us -> 60 us (level)
  no operation moved by 1% of the time
where the time goes in v5:
time: 60 us; the launch traced here: 58.9 us
  Pallas kernels  58.3 us (97%)
  between operations  0.64 us (1%)
    pallas_call x1, Pallas kernels, local(): pl.pallas_call(lambda *refs: kernel(image_total, *refs), out_shape=(pltpu...  57.4 us

profile of v5, /device:TPU:1, one launch (start us, length us, event | category | flops | bytes accessed | tf_op | source)
XLA Modules:
  0.0 58.9 jit_solution(4975255185817895093)
XLA Ops:
  0.6 57.4 %gaussian_stats.1 = (f32[104,16,100]{2,1,0:T(8,128)S(1)}, f32[16,100]{1,0:T(8,128)S(1)}) custom-call(s32[1,100]{1,0:T(1,128)} %bitcast.4, bf16[2,4,448,512]{3,2,1,0:T(8,128)(2,1)} %bitcast.3), custom_call_target="tpu_custom_call" | custom-call | tf_op jit(solution)/shard_map/gaussian_stats/pallas_call | solution.py:319
  58.0 0.9 %store.1 = (f32[100,16,100]{2,1,0:T(8,128)}, f32[16,100]{1,0:T(8,128)}) custom-call(f32[104,16,100]{2,1,0:T(8,128)S(1)} %get-tuple-element.6.factor_in, f32[16,100]{1,0:T(8,128)S(1)} %get-tuple-element.7.mean_in), custom_call_target="tpu_custom_call" | custom-call | tf_op jit(solution)/shard_map/store/pallas_call | solution.py:348
